TPU v7x, 1024 devices: a whole 4x4x32 slice. The times are simulated.
1024 devices in a mesh: clip: 64 (over z, y_hi), seq: 16 (over y_lo, x, core).
Axes of the slice: x: 4, y: 4 (y_hi: 2, y_lo: 2; y = y_hi * 2 + y_lo), z: 32, core: 2. Of those that a mesh axis runs over, the one named last changes fastest.
Arguments:
- features: bfloat16 [3, 64, 2048, 3072], P(None, 'clip', 'seq'), may hold values from -60 to 60
- disc_query: bfloat16 [3, 24, 16, 128], replicated, may hold values from -4 to 4
- value_map: bfloat16 [3, 128, 128], replicated, may hold values from -0.5 to 0.5
- disc_out: bfloat16 [3, 24, 16, 128], replicated, may hold values from -0.5 to 0.5
- label: int32 [64], P('clip'), may hold values from 0 to 1
Outputs:
- logits: float32 [64], P('clip')
- grad_query: float32 [3, 24, 16, 128], P(None, None, 'seq')
- grad_out: float32 [3, 24, 16, 128], P(None, None, 'seq')
- grad_value: float32 [3, 128, 128], P(None, 'seq')
All inputs are finite; a program needn't handle non-finite values.
Results may differ from a plain program's by a relative error of at most 0.0095.
Values sent between devices are 32-bit elements; how exact they have to be, the bound alone decides.
No kernel may reach another device: no remote copies, remote signals or barrier semaphores. Data moves between devices by JAX's collectives and lax.ppermute only.
A program may use at most 64 MiB of HBM per device.

v0:
```python
import math

import jax
import jax.numpy as jnp
from jax import lax
from jax.sharding import PartitionSpec as P


def merged_2(shard, axis, combine):
    everything = jax.tree.map(lambda part: lax.all_gather(part, axis), shard)
    leading = jax.tree.map(lambda part: part[0], everything)

    def step(k, so_far):
        return combine(so_far, jax.tree.map(lambda part: part[k], everything))

    return lax.fori_loop(1, lax.axis_size(axis), step, leading)


def join_stats(earlier, later):
    biggest = jnp.maximum(earlier[0], later[0])
    first_factor = jnp.exp(earlier[0] - biggest)
    second_factor = jnp.exp(later[0] - biggest)
    merged_total = earlier[1] * first_factor + later[1] * second_factor
    merged_acc = earlier[2] * first_factor[..., None] + later[2] * second_factor[..., None]
    return (biggest, merged_total, merged_acc)


def tap_partials(tap_rows, query_tap, map_tap, scaling):
    tokens_here = tap_rows.shape[0]
    heads_count = query_tap.shape[0]
    head_size = query_tap.shape[2]
    split_feats = tap_rows.reshape(tokens_here, heads_count, head_size)
    values_tap = jnp.dot(
        tap_rows.reshape(tokens_here * heads_count, head_size),
        map_tap,
        preferred_element_type=jnp.float32,
    ).astype(jnp.bfloat16)
    values_tap = values_tap.reshape(tokens_here, heads_count, head_size)
    scores = (
        jnp.einsum("hje,the->hjt", query_tap, split_feats, preferred_element_type=jnp.float32)
        * scaling
    )
    local_max = jnp.max(scores, axis=-1)
    weights = jnp.exp(scores - local_max[..., None])
    local_total = jnp.sum(weights, axis=-1)
    local_acc = jnp.einsum(
        "hjt,thf->hjf", weights.astype(jnp.bfloat16), values_tap, preferred_element_type=jnp.float32
    )
    return (split_feats, values_tap, scores, (local_max, local_total, local_acc))


def tap_grads(
    split_feats,
    values_tap,
    scores,
    merged_max,
    merged_total,
    output,
    head_weight,
    gradient_scale,
    scaling,
):
    head_size = split_feats.shape[2]
    upstream = (gradient_scale * head_weight.astype(jnp.float32)).astype(jnp.bfloat16)
    soft_weights = jnp.exp(scores - merged_max[..., None]) / merged_total[..., None]
    value_dots = jnp.einsum(
        "hje,the->hjt", upstream, values_tap, preferred_element_type=jnp.float32
    )
    centre = jnp.sum(output * upstream.astype(jnp.float32), axis=-1)
    slopes = soft_weights * (value_dots - centre[..., None])
    query_grad = scaling * jnp.einsum(
        "hjt,the->hje", slopes.astype(jnp.bfloat16), split_feats, preferred_element_type=jnp.float32
    )
    value_grads = jnp.einsum(
        "hjt,hje->the",
        soft_weights.astype(jnp.bfloat16),
        upstream,
        preferred_element_type=jnp.float32,
    ).astype(jnp.bfloat16)
    map_grad = lax.dot_general(
        split_feats.reshape(-1, head_size),
        value_grads.reshape(-1, head_size),
        (((0,), (0,)), ((), ())),
        preferred_element_type=jnp.float32,
    )
    return (query_grad, map_grad)


def on_device(features, disc_query, value_map, disc_out, label):
    tap_count = features.shape[0]
    head_size = disc_query.shape[3]
    query_rows = disc_query.shape[2]
    scaling = 0.5 / math.sqrt(head_size)
    label_sign = 2.0 * label[0].astype(jnp.float32) - 1.0
    kept_taps = []
    merged_taps = []
    for tap_index in range(tap_count):
        kept_taps.append(
            tap_partials(
                features[tap_index, 0], disc_query[tap_index], value_map[tap_index], scaling
            )
        )
    stat_max = jnp.stack([tap_parts[3][0] for tap_parts in kept_taps])
    stat_total = jnp.stack([tap_parts[3][1] for tap_parts in kept_taps])
    stat_acc = jnp.stack([tap_parts[3][2] for tap_parts in kept_taps])
    merged = merged_2((stat_max, stat_total, stat_acc), "seq", join_stats)
    for tap_index in range(tap_count):
        merged_taps.append((merged[0][tap_index], merged[1][tap_index], merged[2][tap_index]))
    outputs = []
    logit_value = jnp.zeros((), jnp.float32)
    for tap_index in range(tap_count):
        output = merged_taps[tap_index][2] / merged_taps[tap_index][1][..., None]
        outputs.append(output)
        logit_value = logit_value + jnp.sum(output * disc_out[tap_index].astype(jnp.float32))
    gradient_scale = -label_sign * jax.nn.sigmoid(-label_sign * logit_value)
    query_list = []
    map_list = []
    for tap_index in range(tap_count):
        split_feats, values_tap, scores, unused_parts = kept_taps[tap_index]
        query_grad, map_grad = tap_grads(
            split_feats,
            values_tap,
            scores,
            merged_taps[tap_index][0],
            merged_taps[tap_index][1],
            outputs[tap_index],
            disc_out[tap_index],
            gradient_scale,
            scaling,
        )
        query_list.append(query_grad)
        map_list.append(map_grad)
    query_all = jnp.stack(query_list)
    map_all = jnp.stack(map_list)
    out_all = gradient_scale * jnp.stack(outputs)
    seq_count = lax.axis_size("seq")
    seq_index = lax.axis_index("seq")
    query_share = query_rows // seq_count
    map_share = head_size // seq_count
    out_part = lax.dynamic_slice_in_dim(out_all, seq_index * query_share, query_share, 2)
    summed = lax.psum((query_all, map_all), ("clip", "seq"))
    query_part = lax.dynamic_slice_in_dim(summed[0], seq_index * query_share, query_share, 2)
    map_part = lax.dynamic_slice_in_dim(summed[1], seq_index * map_share, map_share, 1)
    out_part = lax.psum(out_part, "clip")
    return (logit_value.reshape(1), query_part, out_part, map_part)


def solution(mesh):
    placed = (P(None, "clip", "seq", None), P(), P(), P(), P("clip"))
    return jax.shard_map(
        on_device,
        mesh=mesh,
        in_specs=placed,
        out_specs=(
            P("clip"),
            P(None, None, "seq", None),
            P(None, None, "seq", None),
            P(None, "seq", None),
        ),
        check_vma=False,
    )
```

profile of v0, /device:TPU:1, one launch (start us, length us, event | category | flops | bytes accessed | tf_op | source)
XLA Modules:
  0.0 1069.3 jit_solution(4162137580464782332)
XLA Ops:
  7.2 1.8 fusion.73
  9.0 1.2 copy.136
  10.5 1.2 copy.135
  12.1 1.2 copy.134
  13.6 1.6 fusion.74
  15.3 1.6 fusion.75
  16.9 1.3 fusion.76
  20.6 0.8 pad_maximum_fusion
  21.6 31.1 %all-gather = f32[48,24,16]{1,2,0:T(8,128)S(1)} all-gather(f32[3,24,16]{1,2,0:T(8,128)S(1)} %copy.101), channel_id=2, replica_groups=mesh['clip'=64,'seq'=16] {'seq'}, dimensions={0}, use_global_device_ids=true | all-gather | bytes 78336 | tf_op jit(solution)/shard_map/all_gather | solution.py:10
  53.5 19.4 %all-gather.1 = f32[48,24,16]{1,2,0:T(8,128)S(1)} all-gather(f32[3,24,16]{1,2,0:T(8,128)S(1)} %copy.102), channel_id=3, replica_groups=mesh['clip'=64,'seq'=16] {'seq'}, dimensions={0}, use_global_device_ids=true | all-gather | bytes 78336 | tf_op jit(solution)/shard_map/all_gather | solution.py:10
  74.3 33.0 %all-gather.5.cloned.1.call-done = f32[48,24,16,128]{3,2,1,0:T(8,128)} async-done(((f32[3,24,16,128]{3,2,1,0:T(8,128)}), f32[48,24,16,128]{3,2,1,0:T(8,128)}) %all-gather.5.cloned.1.call-update) | async-done | bytes 9437200 | tf_op jit(solution)/shard_map/all_gather | solution.py:10
  107.4 1.1 slice.104
  108.5 37.0 %while.19 = (s32[]{:T(128)}, f32[3,24,16]{1,2,0:T(8,128)S(1)}, f32[3,24,16]{1,2,0:T(8,128)S(1)}, f32[3,24,16,128]{3,2,1,0:T(8,128)S(1)}, f32[16,3,24,16]{2,3,1,0...) while((s32[]{:T(128)}, f32[3,24,16]{1,2,0:T(8,128)S(1)}, ...), condition=%wide.region_7.0_spmd, body=%wide.region_6.0_spmd.sunk | while | flops 449285 | bytes 1834135 | solution.py:16
  109.4 1.5 fusion.95
  110.9 0.8 fusion.94
  111.9 1.5 fusion.95
  113.4 0.8 fusion.94
  114.3 1.5 fusion.95
  115.9 0.8 fusion.94
  116.8 1.5 fusion.95
  118.3 0.8 fusion.94
  119.3 1.5 fusion.95
  121.7 1.5 fusion.95
  123.3 0.8 fusion.94
  124.2 1.5 fusion.95
  125.7 0.8 fusion.94
  126.7 1.5 fusion.95
  129.1 1.5 fusion.95
  131.6 1.5 fusion.95
  134.1 1.5 fusion.95
  136.5 1.5 fusion.95
  139.0 1.5 fusion.95
  141.4 1.5 fusion.95
  143.9 1.5 fusion.95
  145.7 1.8 fusion.28
  149.5 1.4 multiply_reduce_fusion.2
  151.0 2.6 fusion.5
  153.6 3.1 fusion.6
  156.8 2.6 fusion.4
  159.3 3.0 fusion.7
  162.4 2.6 fusion.3
  165.0 2.3 fusion.8
  167.3 1.7 copy.126
  171.7 0.8 pad_maximum_fusion.1
  173.5 236.1 %psum.22 = f32[3,24,1,128]{3,2,1,0:T(1,128)} all-reduce(f32[3,24,1,128]{3,2,1,0:T(1,128)S(1)} %fusion.65), channel_id=1, replica_groups=mesh['clip'=64,'seq'=16] {'clip'}, use_global_device_ids=true, to_apply=%region_15.0 | all-reduce | flops 9216 | bytes 73728 | tf_op jit(solution)/shard_map/psum | solution.py:144
  409.6 648.4 %all-reduce.3.cloned.1.call-done = (f32[3,24,16,128]{3,2,1,0:T(8,128)}, f32[3,128,128]{1,2,0:T(8,128)}) async-done(((f32[3,24,16,128]{3,2,1,0:T(8,128)}, f32[3,128,128]{1,2,0:T(8,128)}), (f32[3,24,16,128]{3,2,1,0:T(8,128)}, f32[3,128,128]{1,2,0:T(8,128)})) %all-reduce.3.cloned.1.call-update) | async-done | bytes 786448 | tf_op jit(solution)/shard_map/psum | solution.py:141
  1058.0 1.6 constant_dynamic-slice_fusion.1
  1059.6 1.0 constant_dynamic-slice_fusion
  (101 shorter events, 19.1 us)
Async XLA Ops:
  7.2 100.2 %all-gather.5.cloned.1.call-start = ((), (), s32[]{:S(2)}) async-start(), calls=%async_computation | async-start | bytes 10027008 | tf_op jit(solution)/shard_map/all_gather | solution.py:10
  13.6 3.3 copy-start
  13.6 4.6 copy-start.11
  15.3 37.4 %copy-start.4 = (f32[24,16,128]{2,1,0:T(8,128)}, f32[24,16,128]{2,1,0:T(8,128)S(1)}, u32[]{:S(2)}) copy-start(f32[24,16,128]{2,1,0:T(8,128)S(1)} %get-tuple-element.240) | copy-start | bytes 589828
  18.6 0.9 copy-start.3
  19.0 1.3 copy-start.2
  19.3 1.3 copy-start.1
  21.5 1036.5 %all-reduce.3.cloned.1.call-start = ((), (), s32[]{:S(2)}) async-start(), calls=%async_computation.1 | async-start | bytes 1572864 | tf_op jit(solution)/shard_map/psum | solution.py:141
  52.7 21.6 %copy-start.7 = (f32[48,24,16]{1,2,0:T(8,128)}, f32[48,24,16]{1,2,0:T(8,128)S(1)}, u32[]{:S(2)}) copy-start(f32[48,24,16]{1,2,0:T(8,128)S(1)} %all-gather) | copy-start | bytes 221188
  72.9 0.8 copy-start.8
  167.3 2.2 copy-start.5
  169.5 1.1 copy-start.6
  170.6 0.9 copy-start.9
  170.6 1.0 copy-start.10
Sparse Core Ops, SparseCore 0:
  21.6 85.6 all-gather.4
  173.4 884.5 all-reduce.2
where the time goes:
time: 1070 us
  waiting for transfers between devices  681 us (64%)
  blocking collectives  287 us (27%)
  other arithmetic  40.9 us (4%)
  matrix products  24.2 us (2%)
  between operations  18.1 us (2%)
  local copies, waits for them, and re-layouts  17.6 us (2%)
    psum x1, waiting for transfers between devices, on_device(): summed = lax.psum((query_all, map_all), ('clip', 'seq'))  648 us
    psum x1, blocking collectives, on_device(): out_part = lax.psum(out_part, 'clip')  236 us
    all_gather x2, blocking collectives, merged_2(): everything = jax.tree.map(lambda part: lax.all_gather(part, axis), shard)  50.5 us
    all_gather x1, waiting for transfers between devices, merged_2(): everything = jax.tree.map(lambda part: lax.all_gather(part, axis), shard)  33 us
    add x15, other arithmetic, join_stats(): earlier[2] * first_factor[..., None] + later[2] * second_factor[..., None]  22.6 us
  transfers between devices with their start and end apart: 2, of which 2 were waited for; matrix products, arithmetic and copies ran while one was open for 0% of the time, Pallas kernels for 0%

commit v1 on v0

v1 whole, which is shorter than its diff:
```python
import functools
import math

import jax
import jax.numpy as jnp
from jax import lax
from jax.experimental import pallas as pl
from jax.experimental.pallas import tpu as pltpu
from jax.sharding import Mesh, PartitionSpec as P

LANES = 128
GROUP = 8
F32 = jnp.float32
BF16 = jnp.bfloat16
ROWS_BY_COLUMNS = (((1,), (1,)), ((), ()))
VMEM_LARGE = 16 * 2**20
VMEM_SMALL = 16 * 2**20
ROWS_TO_COLUMNS = (((0,), (1,)), ((), ()))
OVER_ROWS = (((0,), (0,)), ((), ()))


def fetched(feats_hbm, feats, sem, groups, tap, group):
    width = GROUP * LANES
    part = tap * groups + group
    return pltpu.make_async_copy(
        feats_hbm.at[tap, 0, :, pl.ds(group * width, width)], feats.at[part], sem.at[part]
    )


def weights_kernel(
    groups, scaling, core, feats_hbm, query_hbm, map_hbm, weight_hbm, weights, ordered, stats,
    kept, masks, block_diag, feats, query, value_map, out_weight, sem, side_sem,
):
    taps, _, queries, _ = query.shape
    count = taps * groups
    half = LANES // 2
    each = queries // 2
    sides = [
        [
            pltpu.make_async_copy(whole.at[tap], copied.at[tap], side_sem.at[place, tap])
            for place, (whole, copied) in enumerate(((query_hbm, query), (weight_hbm, out_weight), (map_hbm, value_map)))
        ]
        for tap in range(taps)
    ]
    for tap in range(taps):
        for side in sides[tap]:
            side.start()
        for group in range(groups):
            fetched(feats_hbm, feats, sem, groups, tap, group).start()
    kept[...] = jnp.zeros_like(kept)
    mine = core[0]
    row = lax.broadcasted_iota(jnp.int32, (LANES, LANES), 0)
    column = lax.broadcasted_iota(jnp.int32, (LANES, LANES), 1)
    row_head = (row % half) // each
    parity = jnp.where(row < half, mine, 1 - mine)
    order = (column == row_head * queries + 2 * (row % each) + parity).astype(F32).astype(BF16)
    for head in range(GROUP):
        masks[head] = ((column % half) // each == head).astype(F32).astype(BF16)
    for tap in range(taps):
        for side in sides[tap]:
            side.wait()
        for group in range(groups):
            part = tap * groups + group
            heads = pl.ds(group * GROUP, GROUP)
            asked = lax.dot_general(
                query[tap, heads].reshape(LANES, LANES), order, ROWS_TO_COLUMNS, preferred_element_type=F32
            ).astype(BF16)
            wanted = jnp.dot(
                order, out_weight[tap, heads].reshape(LANES, LANES), preferred_element_type=F32
            ).astype(BF16)
            ordered[part] = wanted
            weighed = lax.dot_general(value_map[tap], wanted, ROWS_BY_COLUMNS, preferred_element_type=F32).astype(BF16)
            spread = block_diag.at[part % 3]
            for head in range(GROUP):
                columns = slice(head * LANES, (head + 1) * LANES)
                spread[columns, :LANES] = asked * masks[head]
                spread[columns, LANES:] = weighed * masks[head]
            fetched(feats_hbm, feats, sem, groups, tap, group).wait()
            both = jnp.dot(feats[part], spread[...], preferred_element_type=F32)
            scores = both[:, :LANES] * scaling
            dots = both[:, LANES:]
            top = jnp.max(scores, axis=0, keepdims=True)
            expo = jnp.exp(scores - top)
            total = jnp.sum(expo, axis=0, keepdims=True)
            weighted = jnp.sum(expo * dots, axis=0, keepdims=True)
            tilt = expo * (dots - weighted / total)
            kept[part : part + 1, :] = top
            kept[count + part : count + part + 1, :] = total
            kept[2 * count + part : 2 * count + part + 1, :] = weighted
            weights[part, 0] = expo.T.astype(BF16)
            weights[part, 1] = tilt.T.astype(BF16)
    found = kept[...]
    found = jnp.where(mine == 0, found, pltpu.roll(found, half, 1))
    stats[...] = jnp.broadcast_to(found[None], stats.shape)


def token_weights(core, features, disc_query, value_map, disc_out, scaling, members):
    taps, heads, queries, head_size = disc_query.shape
    groups = heads // GROUP
    tokens = features.shape[2]
    vmem = pl.BlockSpec(memory_space=pltpu.VMEM)
    return pl.pallas_call(
        functools.partial(weights_kernel, groups, scaling),
        out_shape=(
            jax.ShapeDtypeStruct((taps * groups, 2, LANES, tokens), BF16),
            jax.ShapeDtypeStruct((taps * groups, LANES, head_size), BF16),
            jax.ShapeDtypeStruct((members, 32, LANES), F32),
        ),
        in_specs=[pl.BlockSpec(memory_space=pltpu.SMEM)] + [pl.BlockSpec(memory_space=pl.ANY)] * 4,
        out_specs=(vmem, vmem, vmem),
        scratch_shapes=[
            pltpu.VMEM((32, LANES), F32),
            pltpu.VMEM((GROUP, LANES, LANES), BF16),
            pltpu.VMEM((3, GROUP * LANES, 2 * LANES), BF16),
            pltpu.VMEM((taps * groups, tokens, GROUP * LANES), BF16),
            pltpu.VMEM(disc_query.shape, BF16),
            pltpu.VMEM(value_map.shape, BF16),
            pltpu.VMEM(disc_out.shape, BF16),
            pltpu.SemaphoreType.DMA((taps * groups,)),
            pltpu.SemaphoreType.DMA((3, taps)),
        ],
        compiler_params=pltpu.CompilerParams(vmem_limit_bytes=VMEM_LARGE),
        cost_estimate=pl.CostEstimate(flops=7 * 10**8, bytes_accessed=4 * 10**6, transcendentals=10**5),
        name="token_weights",
    )(core, features, disc_query, value_map, disc_out)


def pooled_kernel(groups, feats_hbm, weights, sent, stays, feats, sem):
    count = weights.shape[0]
    taps = count // groups
    half = LANES // 2
    each = half // GROUP
    for tap in range(taps):
        for group in range(groups):
            fetched(feats_hbm, feats, sem, groups, tap, group).start()
    for tap in range(taps):
        for group in range(groups):
            part = tap * groups + group
            fetched(feats_hbm, feats, sem, groups, tap, group).wait()
            for head in range(GROUP):
                first = slice(head * each, (head + 1) * each)
                second = slice(half + head * each, half + (head + 1) * each)
                found = jnp.dot(
                    jnp.concatenate(
                        [weights[part, 0, first], weights[part, 0, second], weights[part, 1, first], weights[part, 1, second]],
                        axis=0,
                    ),
                    feats[part, :, head * LANES : (head + 1) * LANES],
                    preferred_element_type=F32,
                )
                sent[part, 0, first] = found[:each]
                sent[part, 1, first] = found[each : 2 * each]
                stays[part, first] = found[2 * each : 3 * each]
                sent[part, 2, first] = found[3 * each :]


def pooled_features(features, weights, groups):
    count, _, _, tokens = weights.shape
    vmem = pl.BlockSpec(memory_space=pltpu.VMEM)
    return pl.pallas_call(
        functools.partial(pooled_kernel, groups),
        out_shape=(
            jax.ShapeDtypeStruct((count, 3, LANES // 2, LANES), F32),
            jax.ShapeDtypeStruct((count, LANES // 2, LANES), F32),
        ),
        in_specs=[pl.BlockSpec(memory_space=pl.ANY), vmem],
        out_specs=(vmem, vmem),
        scratch_shapes=[
            pltpu.VMEM((count, tokens, GROUP * LANES), BF16),
            pltpu.SemaphoreType.DMA((count,)),
        ],
        compiler_params=pltpu.CompilerParams(vmem_limit_bytes=VMEM_LARGE),
        cost_estimate=pl.CostEstimate(flops=8 * 10**7, bytes_accessed=4 * 10**6, transcendentals=0),
        name="pooled_features",
    )(features, weights)


def joined_kernel(count, member_ref, core, label, every, logit_ref, coefficients):
    half = LANES // 2
    member, mine = member_ref[0], core[0]
    tops = every[:, 0:count]
    top = jnp.max(tops, axis=0)
    factors = jnp.exp(tops - top[None])
    total = jnp.sum(every[:, count : 2 * count] * factors, axis=0)
    centre = jnp.sum(every[:, 2 * count : 3 * count] * factors, axis=0) / total
    logit = jnp.sum(jnp.sum(centre, axis=1, keepdims=True), axis=0, keepdims=True)
    signs = jnp.full((1, 1), 2 * label[0] - 1, jnp.int32).astype(F32)
    slope = -signs * jax.nn.sigmoid(-signs * logit)
    logit_ref[...] = jnp.broadcast_to(logit, logit_ref.shape)
    padding = jnp.zeros((16 - count, LANES), F32)
    for place, of_member in enumerate((member, member + 1 - 2 * mine)):
        seen = every[of_member]
        share = slope * jnp.exp(seen[0:count] - top) / total
        moved = share * (centre - seen[2 * count : 3 * count] / seen[count : 2 * count])
        both = jnp.concatenate([share, padding, moved, padding], axis=0)
        coefficients[place] = jnp.where(mine == 0, both, pltpu.roll(both, half, 1)).T


def joined_stats(member, core, label, every, count):
    vmem = pl.BlockSpec(memory_space=pltpu.VMEM)
    smem = pl.BlockSpec(memory_space=pltpu.SMEM)
    return pl.pallas_call(
        functools.partial(joined_kernel, count),
        out_shape=(
            jax.ShapeDtypeStruct((8, LANES), F32),
            jax.ShapeDtypeStruct((2, LANES, 32), F32),
        ),
        in_specs=[smem, smem, smem, vmem],
        out_specs=(vmem, vmem),
        compiler_params=pltpu.CompilerParams(vmem_limit_bytes=VMEM_SMALL),
        cost_estimate=pl.CostEstimate(flops=10**10, bytes_accessed=10**8, transcendentals=10**5),
        name="joined_stats",
    )(member, core, label, every)


def scaled_kernel(groups, scaling, core, own, stays, other, coefficients, ordered, shares, whole):
    count = own.shape[0]
    taps = count // groups
    heads = groups * GROUP
    head_size = own.shape[3]
    half = LANES // 2
    each = half // GROUP
    mine = core[0]
    own_columns = coefficients[0]
    other_columns = coefficients[1]

    def spread(found, part, second):
        return jnp.broadcast_to(found[second * half : (second + 1) * half, part : part + 1], (half, LANES))

    for tap in range(taps):
        grad = jnp.zeros((head_size, head_size), F32)
        for group in range(groups):
            part = tap * groups + group
            first_pool = spread(own_columns, part, 0) * own[part, 0] + spread(other_columns, part, 0) * other[part, 1]
            second_pool = spread(own_columns, part, 1) * own[part, 1] + spread(other_columns, part, 1) * other[part, 0]
            tilt = scaling * (
                (spread(own_columns, part, 0) * stays[part] - spread(own_columns, 16 + part, 0) * own[part, 0])
                + (spread(other_columns, part, 0) * other[part, 2] - spread(other_columns, 16 + part, 0) * other[part, 1])
            )
            pool = jnp.concatenate([first_pool, second_pool], axis=0)
            high = pool.astype(BF16)
            low = (pool - high.astype(F32)).astype(BF16)
            grad = grad + lax.dot_general(high, ordered[part], OVER_ROWS, preferred_element_type=F32)
            grad = grad + lax.dot_general(low, ordered[part], OVER_ROWS, preferred_element_type=F32)
            row = tap * heads + group * GROUP
            for head in range(GROUP):
                rows = slice(head * each, (head + 1) * each)
                shares[0, :, row + head, :] = tilt[rows]
                shares[1, :, row + head, :] = first_pool[rows]
        pieces = shares.shape[1]
        kept = head_size // (2 * pieces)
        whole[tap] = grad.reshape(whole.shape[1:])
        place, second = divmod(tap, 2)
        row = taps * heads + second * kept
        shares[place, :, row : row + kept, :] = whole[tap, :, mine]
    row = taps * heads + kept
    shares[1, :, row:, :] = jnp.zeros((pieces, kept, head_size), F32)


def scaled_shares(core, own, stays, other, coefficients, ordered, taps, pieces, scaling):
    count, _, _, head_size = own.shape
    groups = count // taps
    kept = head_size // (2 * pieces)
    vmem = pl.BlockSpec(memory_space=pltpu.VMEM)
    smem = pl.BlockSpec(memory_space=pltpu.SMEM)
    rows = count * GROUP + 2 * kept
    return pl.pallas_call(
        functools.partial(scaled_kernel, groups, scaling),
        out_shape=jax.ShapeDtypeStruct((2, pieces, rows, head_size), F32),
        in_specs=[smem, vmem, vmem, vmem, vmem, vmem],
        out_specs=vmem,
        scratch_shapes=[pltpu.VMEM((taps, pieces, 2, kept, head_size), F32)],
        compiler_params=pltpu.CompilerParams(vmem_limit_bytes=VMEM_SMALL),
        cost_estimate=pl.CostEstimate(flops=10**8, bytes_accessed=3 * 10**6, transcendentals=10**5),
        name="scaled_shares",
    )(core, own, stays, other, coefficients, ordered)


def summed_kernel(terms, total):
    found = terms[0]
    for term in range(1, terms.shape[0]):
        found = found + terms[term]
    parts, rows, _ = total.shape
    if parts * rows > found.shape[0]:
        found = jnp.concatenate([found, jnp.zeros((parts * rows - found.shape[0], LANES), F32)], axis=0)
    total[...] = found.reshape(total.shape)


def summed_parts(terms, parts):
    rows = -(-terms.shape[1] // (8 * parts)) * 8
    vmem = pl.BlockSpec(memory_space=pltpu.VMEM)
    return pl.pallas_call(
        summed_kernel,
        out_shape=jax.ShapeDtypeStruct((parts, rows, LANES), F32),
        in_specs=[vmem],
        out_specs=vmem,
        compiler_params=pltpu.CompilerParams(vmem_limit_bytes=VMEM_SMALL),
        name="summed_parts",
    )(terms)


def repeated_kernel(terms, total):
    found = terms[0]
    for term in range(1, terms.shape[0]):
        found = found + terms[term]
    total[...] = jnp.broadcast_to(found[None], total.shape)


def repeated_sum(terms, copies):
    vmem = pl.BlockSpec(memory_space=pltpu.VMEM)
    return pl.pallas_call(
        repeated_kernel,
        out_shape=jax.ShapeDtypeStruct((copies, *terms.shape[1:]), F32),
        in_specs=[vmem],
        out_specs=vmem,
        compiler_params=pltpu.CompilerParams(vmem_limit_bytes=VMEM_SMALL),
        name="repeated_sum",
    )(terms)


def final_kernel(gathered, value_map, query_ref, out_ref, map_ref):
    taps, head_size, _ = value_map.shape
    each = query_ref.shape[0] // taps
    kept = map_ref.shape[1]
    parts = gathered.shape[0]
    first = jnp.concatenate([gathered[part, 0] for part in range(parts)], axis=0)
    second = jnp.concatenate([gathered[part, 1] for part in range(parts)], axis=0)
    query_ref[...] = first[: taps * each]
    for tap in range(taps):
        pool = second[tap * each : (tap + 1) * each]
        high = pool.astype(BF16)
        low = (pool - high.astype(F32)).astype(BF16)
        out_ref[tap * each : (tap + 1) * each, :] = jnp.dot(
            high, value_map[tap], preferred_element_type=F32
        ) + jnp.dot(low, value_map[tap], preferred_element_type=F32)
        row = taps * each + (tap % 2) * kept
        map_ref[tap] = (first, second)[tap // 2][row : row + kept]


def final_outputs(gathered, value_map, heads, kept):
    taps, head_size, _ = value_map.shape
    vmem = pl.BlockSpec(memory_space=pltpu.VMEM)
    each = jax.ShapeDtypeStruct((taps * heads, head_size), F32)
    return pl.pallas_call(
        final_kernel,
        out_shape=(each, each, jax.ShapeDtypeStruct((taps, kept, head_size), F32)),
        in_specs=[vmem, vmem],
        out_specs=(vmem, vmem, vmem),
        compiler_params=pltpu.CompilerParams(vmem_limit_bytes=VMEM_SMALL),
        name="final_outputs",
    )(gathered, value_map)


def exchanged(parts, axes):
    return lax.all_to_all(parts, axes, 0, 0)


SEQ = ("yl", "x", "core")
CLIP = ("zh", "zl", "yh")


def on_device(features, disc_query, value_map, disc_out, label):
    taps, heads, queries, head_size = disc_query.shape
    scaling = 0.5 / math.sqrt(head_size)
    members = lax.axis_size(SEQ)
    core = lax.axis_index("core").astype(jnp.int32).reshape(1)
    member = lax.axis_index(SEQ).astype(jnp.int32).reshape(1)
    features, disc_query, disc_out, map_there = (
        pltpu.with_memory_space_constraint(whole, pltpu.HBM) for whole in (features, disc_query, disc_out, value_map)
    )
    weights, ordered, stats = token_weights(core, features, disc_query, map_there, disc_out, scaling, members)
    every = exchanged(stats, SEQ)
    sent, stays = pooled_features(features, weights, heads // GROUP)
    other = lax.ppermute(sent, "core", [(0, 1), (1, 0)])
    logit, coefficients = joined_stats(member, core, label, every, ordered.shape[0])
    shares = scaled_shares(core, sent, stays, other, coefficients, ordered, taps, members // 2, scaling)
    terms = exchanged(shares.reshape(members, -1, head_size), ("yh", "yl", "x"))
    terms = exchanged(summed_parts(terms, lax.axis_size("zl")), ("zl",))
    terms = exchanged(repeated_sum(terms, lax.axis_size("zh")), ("zh",))
    terms = exchanged(repeated_sum(terms, 2 * lax.axis_size("zl")), ("zl", "yh"))
    gathered = terms.reshape(-1, 2, *terms.shape[1:])
    query_part, out_part, map_part = final_outputs(gathered, value_map, heads, head_size // members)
    return (
        logit[0, :1],
        query_part.reshape(taps, heads, 1, head_size),
        out_part.reshape(taps, heads, 1, head_size),
        map_part,
    )


def solution(mesh):
    clips, members = mesh.shape["clip"], mesh.shape["seq"]
    near = min(4, clips // 2)
    shape = (clips // (2 * near), near, 2, 2, members // 4, 2)
    inner = Mesh(mesh.devices.reshape(shape), (*CLIP, *SEQ))
    placed = (P(None, CLIP, SEQ, None), P(), P(), P(), P(CLIP))
    return jax.shard_map(
        on_device,
        mesh=inner,
        in_specs=placed,
        out_specs=(P(CLIP), P(None, None, SEQ, None), P(None, None, SEQ, None), P(None, SEQ, None)),
        check_vma=False,
    )
```

time: 1070 us -> 117 us (0.11)
  the two profiles are of different devices: /device:TPU:1 before, /device:TPU:4 now
where the time goes in v1:
time: 117 us
  blocking collectives  69.6 us (59%)
  starting transfers between devices  23.3 us (20%)
  Pallas kernels  12.8 us (11%)
  waiting for transfers between devices  9.38 us (8%)
  between operations  1.34 us (1%)
    all_to_all x3, blocking collectives, exchanged(): return lax.all_to_all(parts, axes, 0, 0)  69.6 us
    all_to_all x2, starting transfers between devices, exchanged(): return lax.all_to_all(parts, axes, 0, 0)  21.3 us
    all_to_all x2, waiting for transfers between devices, exchanged(): return lax.all_to_all(parts, axes, 0, 0)  8.12 us
    pallas_call x1, Pallas kernels, token_weights(): pl.pallas_call(functools.partial(weights_kernel, groups, scaling), out_sh...  7.02 us
    pallas_call x1, Pallas kernels, pooled_features(): pl.pallas_call(functools.partial(pooled_kernel, groups), out_shape=(jax.S...  2.7 us
  transfers between devices with their start and end apart: 3, of which 2 were waited for; matrix products, arithmetic and copies ran while one was open for 0% of the time, Pallas kernels for 3%

profile of v1, /device:TPU:4, one launch (start us, length us, event | category | flops | bytes accessed | tf_op | source)
XLA Modules:
  0.0 117.0 jit_solution(3077774692059583934)
XLA Ops:
  0.6 7.0 %token_weights.1 = (bf16[9,2,128,128]{3,2,1,0:T(8,128)(2,1)S(1)}, bf16[9,128,128]{2,1,0:T(8,128)(2,1)S(1)}, f32[16,32,128]{2,1,0:T(8,128)}) custom-call(s32[1]{0:T(128)} %bitcast.1.core, bf16[3,1,128,3072]{3,2,1,0:T(8,128)(2,1)} %feats_hbm.3, bf16[3,24,16,128]{3,2,1,0:T(8,128)(2,1)} %query_hbm.1, bf16[3,128,128]{2,1,0:T(8,128)(2,1)} %value_map.1, ...), custom_call_target="tpu_custom_call" | custom-call | flops 700000000 | bytes 4000000 | tf_op jit(solution)/shard_map/token_weights/pallas_call | solution.py:102
  7.7 16.5 %all-to-all-start = ((f32[16,32,128]{2,1,0:T(8,128)}), f32[16,32,128]{2,1,0:T(8,128)S(1)}, u32[]{:S(2)}, u32[]{:S(2)}) async-start(f32[16,32,128]{2,1,0:T(8,128)} %get-tuple-element.14), calls=%async_computation | async-start | bytes 524288 | tf_op jit(solution)/shard_map/all_to_all | solution.py:355
  24.2 2.7 %pooled_features.1 = (f32[9,3,64,128]{3,2,1,0:T(8,128)S(1)}, f32[9,64,128]{2,1,0:T(8,128)S(1)}) custom-call(bf16[3,1,128,3072]{3,2,1,0:T(8,128)(2,1)} %feats_hbm.3, bf16[9,2,128,128]{3,2,1,0:T(8,128)(2,1)S(1)} %get-tuple-element.16.weights), custom_call_target="tpu_custom_call" | custom-call | flops 80000000 | bytes 4000000 | tf_op jit(solution)/shard_map/pooled_features/pallas_call | solution.py:160
  26.9 2.1 %collective-permute-start = (f32[9,3,64,128]{3,2,1,0:T(8,128)S(1)}, f32[9,3,64,128]{3,2,1,0:T(8,128)S(1)}, u32[]{:S(2)}, u32[]{:S(2)}) collective-permute-start(f32[9,3,64,128]{3,2,1,0:T(8,128)S(1)} %get-tuple-element.17.own), channel_id=1, source_target_pairs={{0,1},{1,0},{2,3},{3,2},{4,5},{5,4},{6,7},{7,6},{8,9},{9,8},{10,11... | collective-permute-start | bytes 2654216 | tf_op jit(solution)/shard_map/ppermute | solution.py:374
  29.6 0.0 all-to-all-done.every
  29.6 0.3 joined_stats.1
  29.9 1.3 %collective-permute-done.other = f32[9,3,64,128]{3,2,1,0:T(8,128)S(1)} collective-permute-done((f32[9,3,64,128]{3,2,1,0:T(8,128)S(1)}, f32[9,3,64,128]{3,2,1,0:T(8,128)S(1)}, u32[]{:S(2)}, u32[]{:S(2)}) %collective-permute-start) | collective-permute-done | bytes 884768 | tf_op jit(solution)/shard_map/ppermute | solution.py:374
  31.2 0.0 copy-start
  31.2 1.3 %scaled_shares.1 = f32[2,8,88,128]{3,2,1,0:T(8,128)S(1)} custom-call(s32[1]{0:T(128)} %bitcast.1.core, f32[9,3,64,128]{3,2,1,0:T(8,128)S(1)} %get-tuple-element.17.own, f32[9,64,128]{2,1,0:T(8,128)S(1)} %get-tuple-element.18.stays, f32[9,3,64,128]{3,2,1,0:T(8,128)S(1)} %collective-permute-done.other, f32[2,128,32]{2,1,0:T(8,128)S(1)} %get-tuple-element.19.coefficients, ...), custom_call_target="tpu_custom_call" | custom-call | flops 100000000 | bytes 3000000 | tf_op jit(solution)/shard_map/scaled_shares/pallas_call | solution.py:267
  32.5 17.2 %all_to_all.25.terms = f32[16,88,128]{2,1,0:T(8,128)S(1)} all-to-all(f32[16,88,128]{2,1,0:T(8,128)S(1)} %bitcast.11), channel_id=1, replica_groups=mesh['zh'=8,'zl'=4,'yh'=2,'yl'=2,'x'=4,'core'=2] {'yh','yl','x'}, dimensions={0} | all-to-all | bytes 1441792 | tf_op jit(solution)/shard_map/all_to_all | solution.py:355
  49.7 8.1 %all_to_all.26.terms = f32[4,24,128]{2,1,0:T(8,128)S(1)} all-to-all(f32[4,24,128]{2,1,0:T(8,128)S(1)} %summed_parts.1), channel_id=1, replica_groups=mesh['zh'=8,'zl'=4,'yh'=2,'yl'=2,'x'=4,'core'=2] {'zl'}, dimensions={0} | all-to-all | bytes 98304 | tf_op jit(solution)/shard_map/all_to_all | solution.py:355
  57.7 44.4 %all_to_all.27.terms = f32[8,24,128]{2,1,0:T(8,128)S(1)} all-to-all(f32[8,24,128]{2,1,0:T(8,128)S(1)} %repeated_sum.2), channel_id=1, replica_groups=mesh['zh'=8,'zl'=4,'yh'=2,'yl'=2,'x'=4,'core'=2] {'zh'}, dimensions={0} | all-to-all | bytes 196608 | tf_op jit(solution)/shard_map/all_to_all | solution.py:355
  102.2 0.7 repeated_sum.3
  102.8 4.8 %all-to-all-start.4 = ((f32[8,24,128]{2,1,0:T(8,128)}), f32[8,24,128]{2,1,0:T(8,128)S(1)}, u32[]{:S(2)}, u32[]{:S(2)}) async-start(f32[8,24,128]{2,1,0:T(8,128)} %repeated_sum.3), calls=%async_computation.4 | async-start | bytes 196608 | tf_op jit(solution)/shard_map/all_to_all | solution.py:355
  107.6 0.5 slice.3
  108.1 8.1 %all-to-all-done.4 = f32[8,24,128]{2,1,0:T(8,128)S(1)} async-done(((f32[8,24,128]{2,1,0:T(8,128)}), f32[8,24,128]{2,1,0:T(8,128)S(1)}, u32[]{:S(2)}, u32[]{:S(2)}) %all-to-all-start.4) | async-done | bytes 98336 | tf_op jit(solution)/shard_map/all_to_all | solution.py:355
  116.2 0.0 copy-done
  116.2 0.8 final_outputs.1
  (2 shorter events, 0.1 us)
Async XLA Ops:
  7.7 21.9 %all-to-all-start = ((f32[16,32,128]{2,1,0:T(8,128)}), f32[16,32,128]{2,1,0:T(8,128)S(1)}, u32[]{:S(2)}, u32[]{:S(2)}) async-start(f32[16,32,128]{2,1,0:T(8,128)} %get-tuple-element.14), calls=%async_computation | async-start | bytes 524288 | tf_op jit(solution)/shard_map/all_to_all | solution.py:355
  26.9 4.3 %collective-permute-start = (f32[9,3,64,128]{3,2,1,0:T(8,128)S(1)}, f32[9,3,64,128]{3,2,1,0:T(8,128)S(1)}, u32[]{:S(2)}, u32[]{:S(2)}) collective-permute-start(f32[9,3,64,128]{3,2,1,0:T(8,128)S(1)} %get-tuple-element.17.own), channel_id=1, source_target_pairs={{0,1},{1,0},{2,3},{3,2},{4,5},{5,4},{6,7},{7,6},{8,9},{9,8},{10,11... | collective-permute-start | bytes 2654216 | tf_op jit(solution)/shard_map/ppermute | solution.py:374
  31.2 85.0 %copy-start = (bf16[3,128,128]{2,1,0:T(8,128)(2,1)S(1)}, bf16[3,128,128]{2,1,0:T(8,128)(2,1)}, u32[]{:S(2)}) copy-start(bf16[3,128,128]{2,1,0:T(8,128)(2,1)} %value_map.1) | copy-start | bytes 294916
  102.8 13.4 %all-to-all-start.4 = ((f32[8,24,128]{2,1,0:T(8,128)}), f32[8,24,128]{2,1,0:T(8,128)S(1)}, u32[]{:S(2)}, u32[]{:S(2)}) async-start(f32[8,24,128]{2,1,0:T(8,128)} %repeated_sum.3), calls=%async_computation.4 | async-start | bytes 196608 | tf_op jit(solution)/shard_map/all_to_all | solution.py:355

commit v2 on v1

--- a/solution.py
+++ b/solution.py
@@ -13,6 +13,7 @@
 F32 = jnp.float32
 BF16 = jnp.bfloat16
 ROWS_BY_COLUMNS = (((1,), (1,)), ((), ()))
+AHEAD = 3
 VMEM_LARGE = 16 * 2**20
 VMEM_SMALL = 16 * 2**20
 ROWS_TO_COLUMNS = (((0,), (1,)), ((), ()))
@@ -45,6 +46,7 @@
     for tap in range(taps):
         for side in sides[tap]:
             side.start()
+    for tap in range(taps):
         for group in range(groups):
             fetched(feats_hbm, feats, sem, groups, tap, group).start()
     kept[...] = jnp.zeros_like(kept)
@@ -56,39 +58,46 @@
     order = (column == row_head * queries + 2 * (row % each) + parity).astype(F32).astype(BF16)
     for head in range(GROUP):
         masks[head] = ((column % half) // each == head).astype(F32).astype(BF16)
+    def prepare(part):
+        tap, group = divmod(part, groups)
+        heads = pl.ds(group * GROUP, GROUP)
+        asked = lax.dot_general(
+            query[tap, heads].reshape(LANES, LANES), order, ROWS_TO_COLUMNS, preferred_element_type=F32
+        ).astype(BF16)
+        wanted = jnp.dot(
+            order, out_weight[tap, heads].reshape(LANES, LANES), preferred_element_type=F32
+        ).astype(BF16)
+        ordered[part] = wanted
+        weighed = lax.dot_general(value_map[tap], wanted, ROWS_BY_COLUMNS, preferred_element_type=F32).astype(BF16)
+        spread = block_diag.at[part % 3]
+        for head in range(GROUP):
+            rows = slice(head * LANES, (head + 1) * LANES)
+            spread[rows, :LANES] = asked * masks[head]
+            spread[rows, LANES:] = weighed * masks[head]
+
     for tap in range(taps):
         for side in sides[tap]:
             side.wait()
-        for group in range(groups):
-            part = tap * groups + group
-            heads = pl.ds(group * GROUP, GROUP)
-            asked = lax.dot_general(
-                query[tap, heads].reshape(LANES, LANES), order, ROWS_TO_COLUMNS, preferred_element_type=F32
-            ).astype(BF16)
-            wanted = jnp.dot(
-                order, out_weight[tap, heads].reshape(LANES, LANES), preferred_element_type=F32
-            ).astype(BF16)
-            ordered[part] = wanted
-            weighed = lax.dot_general(value_map[tap], wanted, ROWS_BY_COLUMNS, preferred_element_type=F32).astype(BF16)
-            spread = block_diag.at[part % 3]
-            for head in range(GROUP):
-                columns = slice(head * LANES, (head + 1) * LANES)
-                spread[columns, :LANES] = asked * masks[head]
-                spread[columns, LANES:] = weighed * masks[head]
-            fetched(feats_hbm, feats, sem, groups, tap, group).wait()
-            both = jnp.dot(feats[part], spread[...], preferred_element_type=F32)
-            scores = both[:, :LANES] * scaling
-            dots = both[:, LANES:]
-            top = jnp.max(scores, axis=0, keepdims=True)
-            expo = jnp.exp(scores - top)
-            total = jnp.sum(expo, axis=0, keepdims=True)
-            weighted = jnp.sum(expo * dots, axis=0, keepdims=True)
-            tilt = expo * (dots - weighted / total)
-            kept[part : part + 1, :] = top
-            kept[count + part : count + part + 1, :] = total
-            kept[2 * count + part : 2 * count + part + 1, :] = weighted
-            weights[part, 0] = expo.T.astype(BF16)
-            weights[part, 1] = tilt.T.astype(BF16)
+    for part in range(AHEAD):
+        prepare(part)
+    for part in range(count):
+        fetched(feats_hbm, feats, sem, groups, *divmod(part, groups)).wait()
+    for part in range(count):
+        both = jnp.dot(feats[part], block_diag[part % 3], preferred_element_type=F32)
+        if part + AHEAD < count:
+            prepare(part + AHEAD)
+        scores = both[:, :LANES] * scaling
+        dots = both[:, LANES:]
+        top = jnp.max(scores, axis=0, keepdims=True)
+        expo = jnp.exp(scores - top)
+        total = jnp.sum(expo, axis=0, keepdims=True)
+        weighted = jnp.sum(expo * dots, axis=0, keepdims=True)
+        tilt = expo * (dots - weighted / total)
+        kept[part : part + 1, :] = top
+        kept[count + part : count + part + 1, :] = total
+        kept[2 * count + part : 2 * count + part + 1, :] = weighted
+        weights[part, :, :LANES] = expo.astype(BF16)
+        weights[part, :, LANES:] = tilt.astype(BF16)
     found = kept[...]
     found = jnp.where(mine == 0, found, pltpu.roll(found, half, 1))
     stats[...] = jnp.broadcast_to(found[None], stats.shape)
@@ -102,7 +111,7 @@
     return pl.pallas_call(
         functools.partial(weights_kernel, groups, scaling),
         out_shape=(
-            jax.ShapeDtypeStruct((taps * groups, 2, LANES, tokens), BF16),
+            jax.ShapeDtypeStruct((taps * groups, tokens, 2 * LANES), BF16),
             jax.ShapeDtypeStruct((taps * groups, LANES, head_size), BF16),
             jax.ShapeDtypeStruct((members, 32, LANES), F32),
         ),
@@ -135,14 +144,17 @@
             fetched(feats_hbm, feats, sem, groups, tap, group).start()
     for tap in range(taps):
         for group in range(groups):
+            fetched(feats_hbm, feats, sem, groups, tap, group).wait()
+    for tap in range(taps):
+        for group in range(groups):
             part = tap * groups + group
-            fetched(feats_hbm, feats, sem, groups, tap, group).wait()
+            rows = weights[part].T
             for head in range(GROUP):
                 first = slice(head * each, (head + 1) * each)
                 second = slice(half + head * each, half + (head + 1) * each)
                 found = jnp.dot(
                     jnp.concatenate(
-                        [weights[part, 0, first], weights[part, 0, second], weights[part, 1, first], weights[part, 1, second]],
+                        [rows[LANES * kind + half * place + head * each :][:each] for kind in range(2) for place in range(2)],
                         axis=0,
                     ),
                     feats[part, :, head * LANES : (head + 1) * LANES],
@@ -155,7 +167,7 @@
 
 
 def pooled_features(features, weights, groups):
-    count, _, _, tokens = weights.shape
+    count, tokens, _ = weights.shape
     vmem = pl.BlockSpec(memory_space=pltpu.VMEM)
     return pl.pallas_call(
         functools.partial(pooled_kernel, groups),
@@ -186,7 +198,7 @@
     logit = jnp.sum(jnp.sum(centre, axis=1, keepdims=True), axis=0, keepdims=True)
     signs = jnp.full((1, 1), 2 * label[0] - 1, jnp.int32).astype(F32)
     slope = -signs * jax.nn.sigmoid(-signs * logit)
-    logit_ref[...] = jnp.broadcast_to(logit, logit_ref.shape)
+    logit_ref[...] = logit
     padding = jnp.zeros((16 - count, LANES), F32)
     for place, of_member in enumerate((member, member + 1 - 2 * mine)):
         seen = every[of_member]
@@ -202,7 +214,7 @@
     return pl.pallas_call(
         functools.partial(joined_kernel, count),
         out_shape=(
-            jax.ShapeDtypeStruct((8, LANES), F32),
+            jax.ShapeDtypeStruct((1, 1), F32),
             jax.ShapeDtypeStruct((2, LANES, 32), F32),
         ),
         in_specs=[smem, smem, smem, vmem],
@@ -381,7 +393,7 @@
     gathered = terms.reshape(-1, 2, *terms.shape[1:])
     query_part, out_part, map_part = final_outputs(gathered, value_map, heads, head_size // members)
     return (
-        logit[0, :1],
+        logit.reshape(1),
         query_part.reshape(taps, heads, 1, head_size),
         out_part.reshape(taps, heads, 1, head_size),
         map_part,

time: 117 us -> 114 us (0.974)
  the two profiles are of different devices: /device:TPU:4 before, /device:TPU:8 now
where the time goes in v2:
time: 114 us
  blocking collectives  82.3 us (72%)
  starting transfers between devices  18.5 us (16%)
  Pallas kernels  10.3 us (9%)
  between operations  1.34 us (1%)
  waiting for transfers between devices  1.32 us (1%)
    all_to_all x4, blocking collectives, exchanged(): return lax.all_to_all(parts, axes, 0, 0)  82.3 us
    all_to_all x1, starting transfers between devices, exchanged(): return lax.all_to_all(parts, axes, 0, 0)  16.5 us
    pallas_call x1, Pallas kernels, token_weights(): pl.pallas_call(functools.partial(weights_kernel, groups, scaling), out_sh...  5.06 us
    pallas_call x1, Pallas kernels, pooled_features(): pl.pallas_call(functools.partial(pooled_kernel, groups), out_shape=(jax.S...  2.44 us
  transfers between devices with their start and end apart: 2, of which 1 were waited for; matrix products, arithmetic and copies ran while one was open for 0% of the time, Pallas kernels for 3%

profile of v2, /device:TPU:8, one launch (start us, length us, event | category | flops | bytes accessed | tf_op | source)
XLA Modules:
  0.0 113.8 jit_solution(16249215197054602231)
XLA Ops:
  0.6 5.1 %token_weights.1 = (bf16[9,128,256]{2,1,0:T(8,128)(2,1)S(1)}, bf16[9,128,128]{2,1,0:T(8,128)(2,1)S(1)}, f32[16,32,128]{2,1,0:T(8,128)}) custom-call(s32[1]{0:T(128)} %bitcast.1.core, bf16[3,1,128,3072]{3,2,1,0:T(8,128)(2,1)} %feats_hbm.3, bf16[3,24,16,128]{3,2,1,0:T(8,128)(2,1)} %query_hbm.1, bf16[3,128,128]{2,1,0:T(8,128)(2,1)} %value_map.1, ...), custom_call_target="tpu_custom_call" | custom-call | flops 700000000 | bytes 4000000 | tf_op jit(solution)/shard_map/token_weights/pallas_call | solution.py:111
  5.7 16.5 %all-to-all-start = ((f32[16,32,128]{2,1,0:T(8,128)}), f32[16,32,128]{2,1,0:T(8,128)S(1)}, u32[]{:S(2)}, u32[]{:S(2)}) async-start(f32[16,32,128]{2,1,0:T(8,128)} %get-tuple-element.14), calls=%async_computation | async-start | bytes 524288 | tf_op jit(solution)/shard_map/all_to_all | solution.py:367
  22.2 2.4 %pooled_features.1 = (f32[9,3,64,128]{3,2,1,0:T(8,128)S(1)}, f32[9,64,128]{2,1,0:T(8,128)S(1)}) custom-call(bf16[3,1,128,3072]{3,2,1,0:T(8,128)(2,1)} %feats_hbm.3, bf16[9,128,256]{2,1,0:T(8,128)(2,1)S(1)} %get-tuple-element.16.weights), custom_call_target="tpu_custom_call" | custom-call | flops 80000000 | bytes 4000000 | tf_op jit(solution)/shard_map/pooled_features/pallas_call | solution.py:172
  24.6 2.1 %collective-permute-start = (f32[9,3,64,128]{3,2,1,0:T(8,128)S(1)}, f32[9,3,64,128]{3,2,1,0:T(8,128)S(1)}, u32[]{:S(2)}, u32[]{:S(2)}) collective-permute-start(f32[9,3,64,128]{3,2,1,0:T(8,128)S(1)} %get-tuple-element.17.own), channel_id=1, source_target_pairs={{0,1},{1,0},{2,3},{3,2},{4,5},{5,4},{6,7},{7,6},{8,9},{9,8},{10,11... | collective-permute-start | bytes 2654216 | tf_op jit(solution)/shard_map/ppermute | solution.py:386
  27.4 1.3 %all-to-all-done.every = f32[16,32,128]{2,1,0:T(8,128)S(1)} async-done(((f32[16,32,128]{2,1,0:T(8,128)}), f32[16,32,128]{2,1,0:T(8,128)S(1)}, u32[]{:S(2)}, u32[]{:S(2)}) %all-to-all-start) | async-done | bytes 262176 | tf_op jit(solution)/shard_map/all_to_all | solution.py:367
  28.7 0.7 joined_stats.1
  29.3 0.0 collective-permute-done.other
  29.3 0.0 copy-start
  29.3 1.3 %scaled_shares.1 = f32[2,8,88,128]{3,2,1,0:T(8,128)S(1)} custom-call(s32[1]{0:T(128)} %bitcast.1.core, f32[9,3,64,128]{3,2,1,0:T(8,128)S(1)} %get-tuple-element.17.own, f32[9,64,128]{2,1,0:T(8,128)S(1)} %get-tuple-element.18.stays, f32[9,3,64,128]{3,2,1,0:T(8,128)S(1)} %collective-permute-done.other, f32[2,128,32]{2,1,0:T(8,128)S(1)} %get-tuple-element.19.coefficients, ...), custom_call_target="tpu_custom_call" | custom-call | flops 100000000 | bytes 3000000 | tf_op jit(solution)/shard_map/scaled_shares/pallas_call | solution.py:279
  30.6 17.1 %all_to_all.25.terms = f32[16,88,128]{2,1,0:T(8,128)S(1)} all-to-all(f32[16,88,128]{2,1,0:T(8,128)S(1)} %bitcast.11), channel_id=1, replica_groups=mesh['zh'=8,'zl'=4,'yh'=2,'yl'=2,'x'=4,'core'=2] {'yh','yl','x'}, dimensions={0} | all-to-all | bytes 1441792 | tf_op jit(solution)/shard_map/all_to_all | solution.py:367
  47.8 8.1 %all_to_all.26.terms = f32[4,24,128]{2,1,0:T(8,128)S(1)} all-to-all(f32[4,24,128]{2,1,0:T(8,128)S(1)} %summed_parts.1), channel_id=1, replica_groups=mesh['zh'=8,'zl'=4,'yh'=2,'yl'=2,'x'=4,'core'=2] {'zl'}, dimensions={0} | all-to-all | bytes 98304 | tf_op jit(solution)/shard_map/all_to_all | solution.py:367
  55.8 43.5 %all_to_all.27.terms = f32[8,24,128]{2,1,0:T(8,128)S(1)} all-to-all(f32[8,24,128]{2,1,0:T(8,128)S(1)} %repeated_sum.2), channel_id=1, replica_groups=mesh['zh'=8,'zl'=4,'yh'=2,'yl'=2,'x'=4,'core'=2] {'zh'}, dimensions={0} | all-to-all | bytes 196608 | tf_op jit(solution)/shard_map/all_to_all | solution.py:367
  99.4 13.6 %all_to_all.28 = f32[8,24,128]{2,1,0:T(8,128)S(1)} all-to-all(f32[8,24,128]{2,1,0:T(8,128)S(1)} %repeated_sum.3), channel_id=1, replica_groups=mesh['zh'=8,'zl'=4,'yh'=2,'yl'=2,'x'=4,'core'=2] {'zl','yh'}, dimensions={0} | all-to-all | bytes 196608 | tf_op jit(solution)/shard_map/all_to_all | solution.py:367
  113.0 0.0 copy-done
  113.0 0.8 final_outputs.1
  (3 shorter events, 0.1 us)
Async XLA Ops:
  5.7 23.0 %all-to-all-start = ((f32[16,32,128]{2,1,0:T(8,128)}), f32[16,32,128]{2,1,0:T(8,128)S(1)}, u32[]{:S(2)}, u32[]{:S(2)}) async-start(f32[16,32,128]{2,1,0:T(8,128)} %get-tuple-element.14), calls=%async_computation | async-start | bytes 524288 | tf_op jit(solution)/shard_map/all_to_all | solution.py:367
  24.6 4.7 %collective-permute-start = (f32[9,3,64,128]{3,2,1,0:T(8,128)S(1)}, f32[9,3,64,128]{3,2,1,0:T(8,128)S(1)}, u32[]{:S(2)}, u32[]{:S(2)}) collective-permute-start(f32[9,3,64,128]{3,2,1,0:T(8,128)S(1)} %get-tuple-element.17.own), channel_id=1, source_target_pairs={{0,1},{1,0},{2,3},{3,2},{4,5},{5,4},{6,7},{7,6},{8,9},{9,8},{10,11... | collective-permute-start | bytes 2654216 | tf_op jit(solution)/shard_map/ppermute | solution.py:386
  29.3 83.7 %copy-start = (bf16[3,128,128]{2,1,0:T(8,128)(2,1)S(1)}, bf16[3,128,128]{2,1,0:T(8,128)(2,1)}, u32[]{:S(2)}) copy-start(bf16[3,128,128]{2,1,0:T(8,128)(2,1)} %value_map.1) | copy-start | bytes 294916

commit v3 on v2

--- a/solution.py
+++ b/solution.py
@@ -388,7 +388,7 @@
     shares = scaled_shares(core, sent, stays, other, coefficients, ordered, taps, members // 2, scaling)
     terms = exchanged(shares.reshape(members, -1, head_size), ("yh", "yl", "x"))
     terms = exchanged(summed_parts(terms, lax.axis_size("zl")), ("zl",))
-    terms = exchanged(repeated_sum(terms, lax.axis_size("zh")), ("zh",))
+    terms = lax.all_gather(repeated_sum(terms, 1)[0], "zh")
     terms = exchanged(repeated_sum(terms, 2 * lax.axis_size("zl")), ("zl", "yh"))
     gathered = terms.reshape(-1, 2, *terms.shape[1:])
     query_part, out_part, map_part = final_outputs(gathered, value_map, heads, head_size // members)

time: 114 us -> 113 us (level)
  blocking collectives: 82.3 us -> 81 us
    all_to_all x4 -> x3, blocking collectives: 82.3 us -> 37.3 us  [exchanged(): return lax.all_to_all(parts, axes, 0, 0)]
    all_gather x0 -> x1, blocking collectives: none -> 43.7 us  [on_device(): terms = lax.all_gather(repeated_sum(terms, 1)[0], 'zh')]
where the time goes in v3:
time: 113 us; the launch traced here: 112 us
  blocking collectives  81 us (72%)
  starting transfers between devices  18.5 us (16%)
  Pallas kernels  10.3 us (9%)
  between operations  1.33 us (1%)
  waiting for transfers between devices  1.32 us (1%)
    all_gather x1, blocking collectives, on_device(): terms = lax.all_gather(repeated_sum(terms, 1)[0], 'zh')  43.7 us
    all_to_all x3, blocking collectives, exchanged(): return lax.all_to_all(parts, axes, 0, 0)  37.3 us
    all_to_all x1, starting transfers between devices, exchanged(): return lax.all_to_all(parts, axes, 0, 0)  16.5 us
    pallas_call x1, Pallas kernels, token_weights(): pl.pallas_call(functools.partial(weights_kernel, groups, scaling), out_sh...  5.06 us
    pallas_call x1, Pallas kernels, pooled_features(): pl.pallas_call(functools.partial(pooled_kernel, groups), out_shape=(jax.S...  2.44 us
  transfers between devices with their start and end apart: 2, of which 1 were waited for; matrix products, arithmetic and copies ran while one was open for 0% of the time, Pallas kernels for 3%

profile of v3, /device:TPU:8, one launch (start us, length us, event | category | flops | bytes accessed | tf_op | source)
XLA Modules:
  0.0 112.5 jit_solution(14398629969679667659)
XLA Ops:
  0.6 5.1 %token_weights.1 = (bf16[9,128,256]{2,1,0:T(8,128)(2,1)S(1)}, bf16[9,128,128]{2,1,0:T(8,128)(2,1)S(1)}, f32[16,32,128]{2,1,0:T(8,128)}) custom-call(s32[1]{0:T(128)} %bitcast.1.core, bf16[3,1,128,3072]{3,2,1,0:T(8,128)(2,1)} %feats_hbm.3, bf16[3,24,16,128]{3,2,1,0:T(8,128)(2,1)} %query_hbm.1, bf16[3,128,128]{2,1,0:T(8,128)(2,1)} %value_map.1, ...), custom_call_target="tpu_custom_call" | custom-call | flops 700000000 | bytes 4000000 | tf_op jit(solution)/shard_map/token_weights/pallas_call | solution.py:111
  5.7 16.5 %all-to-all-start = ((f32[16,32,128]{2,1,0:T(8,128)}), f32[16,32,128]{2,1,0:T(8,128)S(1)}, u32[]{:S(2)}, u32[]{:S(2)}) async-start(f32[16,32,128]{2,1,0:T(8,128)} %get-tuple-element.14), calls=%async_computation | async-start | bytes 524288 | tf_op jit(solution)/shard_map/all_to_all | solution.py:367
  22.2 2.4 %pooled_features.1 = (f32[9,3,64,128]{3,2,1,0:T(8,128)S(1)}, f32[9,64,128]{2,1,0:T(8,128)S(1)}) custom-call(bf16[3,1,128,3072]{3,2,1,0:T(8,128)(2,1)} %feats_hbm.3, bf16[9,128,256]{2,1,0:T(8,128)(2,1)S(1)} %get-tuple-element.16.weights), custom_call_target="tpu_custom_call" | custom-call | flops 80000000 | bytes 4000000 | tf_op jit(solution)/shard_map/pooled_features/pallas_call | solution.py:172
  24.6 2.1 %collective-permute-start = (f32[9,3,64,128]{3,2,1,0:T(8,128)S(1)}, f32[9,3,64,128]{3,2,1,0:T(8,128)S(1)}, u32[]{:S(2)}, u32[]{:S(2)}) collective-permute-start(f32[9,3,64,128]{3,2,1,0:T(8,128)S(1)} %get-tuple-element.17.own), channel_id=1, source_target_pairs={{0,1},{1,0},{2,3},{3,2},{4,5},{5,4},{6,7},{7,6},{8,9},{9,8},{10,11... | collective-permute-start | bytes 2654216 | tf_op jit(solution)/shard_map/ppermute | solution.py:386
  27.4 1.3 %all-to-all-done.every = f32[16,32,128]{2,1,0:T(8,128)S(1)} async-done(((f32[16,32,128]{2,1,0:T(8,128)}), f32[16,32,128]{2,1,0:T(8,128)S(1)}, u32[]{:S(2)}, u32[]{:S(2)}) %all-to-all-start) | async-done | bytes 262176 | tf_op jit(solution)/shard_map/all_to_all | solution.py:367
  28.7 0.7 joined_stats.1
  29.3 0.0 collective-permute-done.other
  29.3 0.0 copy-start
  29.3 1.3 %scaled_shares.1 = f32[2,8,88,128]{3,2,1,0:T(8,128)S(1)} custom-call(s32[1]{0:T(128)} %bitcast.1.core, f32[9,3,64,128]{3,2,1,0:T(8,128)S(1)} %get-tuple-element.17.own, f32[9,64,128]{2,1,0:T(8,128)S(1)} %get-tuple-element.18.stays, f32[9,3,64,128]{3,2,1,0:T(8,128)S(1)} %collective-permute-done.other, f32[2,128,32]{2,1,0:T(8,128)S(1)} %get-tuple-element.19.coefficients, ...), custom_call_target="tpu_custom_call" | custom-call | flops 100000000 | bytes 3000000 | tf_op jit(solution)/shard_map/scaled_shares/pallas_call | solution.py:279
  30.6 17.1 %all_to_all.20.terms = f32[16,88,128]{2,1,0:T(8,128)S(1)} all-to-all(f32[16,88,128]{2,1,0:T(8,128)S(1)} %bitcast.11), channel_id=1, replica_groups=mesh['zh'=8,'zl'=4,'yh'=2,'yl'=2,'x'=4,'core'=2] {'yh','yl','x'}, dimensions={0} | all-to-all | bytes 1441792 | tf_op jit(solution)/shard_map/all_to_all | solution.py:367
  47.8 8.1 %all_to_all.21.terms = f32[4,24,128]{2,1,0:T(8,128)S(1)} all-to-all(f32[4,24,128]{2,1,0:T(8,128)S(1)} %summed_parts.1), channel_id=1, replica_groups=mesh['zh'=8,'zl'=4,'yh'=2,'yl'=2,'x'=4,'core'=2] {'zl'}, dimensions={0} | all-to-all | bytes 98304 | tf_op jit(solution)/shard_map/all_to_all | solution.py:367
  55.8 43.7 %all_gather.3.terms = f32[8,24,128]{2,1,0:T(8,128)S(1)} all-gather(f32[1,24,128]{2,1,0:T(8,128)S(1)} %repeated_sum.2), channel_id=1, replica_groups=mesh['zh'=8,'zl'=4,'yh'=2,'yl'=2,'x'=4,'core'=2] {'zh'}, dimensions={0}, use_global_device_ids=true | all-gather | bytes 110592 | tf_op jit(solution)/shard_map/all_gather | solution.py:391
  99.5 12.2 %all_to_all.22 = f32[8,24,128]{2,1,0:T(8,128)S(1)} all-to-all(f32[8,24,128]{2,1,0:T(8,128)S(1)} %repeated_sum.3), channel_id=1, replica_groups=mesh['zh'=8,'zl'=4,'yh'=2,'yl'=2,'x'=4,'core'=2] {'zl','yh'}, dimensions={0} | all-to-all | bytes 196608 | tf_op jit(solution)/shard_map/all_to_all | solution.py:367
  111.7 0.0 copy-done
  111.7 0.8 final_outputs.1
  (3 shorter events, 0.1 us)
Async XLA Ops:
  5.7 23.0 %all-to-all-start = ((f32[16,32,128]{2,1,0:T(8,128)}), f32[16,32,128]{2,1,0:T(8,128)S(1)}, u32[]{:S(2)}, u32[]{:S(2)}) async-start(f32[16,32,128]{2,1,0:T(8,128)} %get-tuple-element.14), calls=%async_computation | async-start | bytes 524288 | tf_op jit(solution)/shard_map/all_to_all | solution.py:367
  24.6 4.7 %collective-permute-start = (f32[9,3,64,128]{3,2,1,0:T(8,128)S(1)}, f32[9,3,64,128]{3,2,1,0:T(8,128)S(1)}, u32[]{:S(2)}, u32[]{:S(2)}) collective-permute-start(f32[9,3,64,128]{3,2,1,0:T(8,128)S(1)} %get-tuple-element.17.own), channel_id=1, source_target_pairs={{0,1},{1,0},{2,3},{3,2},{4,5},{5,4},{6,7},{7,6},{8,9},{9,8},{10,11... | collective-permute-start | bytes 2654216 | tf_op jit(solution)/shard_map/ppermute | solution.py:386
  29.3 82.4 %copy-start = (bf16[3,128,128]{2,1,0:T(8,128)(2,1)S(1)}, bf16[3,128,128]{2,1,0:T(8,128)(2,1)}, u32[]{:S(2)}) copy-start(bf16[3,128,128]{2,1,0:T(8,128)(2,1)} %value_map.1) | copy-start | bytes 294916

commit v4 on v3

--- a/solution.py
+++ b/solution.py
@@ -29,7 +29,7 @@
 
 
 def weights_kernel(
-    groups, scaling, core, feats_hbm, query_hbm, map_hbm, weight_hbm, weights, ordered, stats,
+    groups, scaling, member, label, feats_hbm, query_hbm, map_hbm, weight_hbm, weights, ordered, stats,
     kept, masks, block_diag, feats, query, value_map, out_weight, sem, side_sem,
 ):
     taps, _, queries, _ = query.shape
@@ -50,7 +50,7 @@
         for group in range(groups):
             fetched(feats_hbm, feats, sem, groups, tap, group).start()
     kept[...] = jnp.zeros_like(kept)
-    mine = core[0]
+    mine = lax.rem(member[0], 2)
     row = lax.broadcasted_iota(jnp.int32, (LANES, LANES), 0)
     column = lax.broadcasted_iota(jnp.int32, (LANES, LANES), 1)
     row_head = (row % half) // each
@@ -103,7 +103,7 @@
     stats[...] = jnp.broadcast_to(found[None], stats.shape)
 
 
-def token_weights(core, features, disc_query, value_map, disc_out, scaling, members):
+def token_weights(member, label, features, disc_query, value_map, disc_out, scaling, members):
     taps, heads, queries, head_size = disc_query.shape
     groups = heads // GROUP
     tokens = features.shape[2]
@@ -115,7 +115,7 @@
             jax.ShapeDtypeStruct((taps * groups, LANES, head_size), BF16),
             jax.ShapeDtypeStruct((members, 32, LANES), F32),
         ),
-        in_specs=[pl.BlockSpec(memory_space=pltpu.SMEM)] + [pl.BlockSpec(memory_space=pl.ANY)] * 4,
+        in_specs=[pl.BlockSpec(memory_space=pltpu.SMEM)] * 2 + [pl.BlockSpec(memory_space=pl.ANY)] * 4,
         out_specs=(vmem, vmem, vmem),
         scratch_shapes=[
             pltpu.VMEM((32, LANES), F32),
@@ -131,7 +131,7 @@
         compiler_params=pltpu.CompilerParams(vmem_limit_bytes=VMEM_LARGE),
         cost_estimate=pl.CostEstimate(flops=7 * 10**8, bytes_accessed=4 * 10**6, transcendentals=10**5),
         name="token_weights",
-    )(core, features, disc_query, value_map, disc_out)
+    )(member, label, features, disc_query, value_map, disc_out)
 
 
 def pooled_kernel(groups, feats_hbm, weights, sent, stays, feats, sem):
@@ -187,9 +187,10 @@
     )(features, weights)
 
 
-def joined_kernel(count, member_ref, core, label, every, logit_ref, coefficients):
+def joined_kernel(count, member_ref, label, every, logit_ref, coefficients):
     half = LANES // 2
-    member, mine = member_ref[0], core[0]
+    member = member_ref[0]
+    mine = lax.rem(member, 2)
     tops = every[:, 0:count]
     top = jnp.max(tops, axis=0)
     factors = jnp.exp(tops - top[None])
@@ -208,7 +209,7 @@
         coefficients[place] = jnp.where(mine == 0, both, pltpu.roll(both, half, 1)).T
 
 
-def joined_stats(member, core, label, every, count):
+def joined_stats(member, label, every, count):
     vmem = pl.BlockSpec(memory_space=pltpu.VMEM)
     smem = pl.BlockSpec(memory_space=pltpu.SMEM)
     return pl.pallas_call(
@@ -217,22 +218,22 @@
             jax.ShapeDtypeStruct((1, 1), F32),
             jax.ShapeDtypeStruct((2, LANES, 32), F32),
         ),
-        in_specs=[smem, smem, smem, vmem],
+        in_specs=[smem, smem, vmem],
         out_specs=(vmem, vmem),
         compiler_params=pltpu.CompilerParams(vmem_limit_bytes=VMEM_SMALL),
         cost_estimate=pl.CostEstimate(flops=10**10, bytes_accessed=10**8, transcendentals=10**5),
         name="joined_stats",
-    )(member, core, label, every)
-
-
-def scaled_kernel(groups, scaling, core, own, stays, other, coefficients, ordered, shares, whole):
+    )(member, label, every)
+
+
+def scaled_kernel(groups, scaling, member, own, stays, other, coefficients, ordered, shares, whole):
     count = own.shape[0]
     taps = count // groups
     heads = groups * GROUP
     head_size = own.shape[3]
     half = LANES // 2
     each = half // GROUP
-    mine = core[0]
+    mine = lax.rem(member[0], 2)
     own_columns = coefficients[0]
     other_columns = coefficients[1]
 
@@ -269,7 +270,7 @@
     shares[1, :, row:, :] = jnp.zeros((pieces, kept, head_size), F32)
 
 
-def scaled_shares(core, own, stays, other, coefficients, ordered, taps, pieces, scaling):
+def scaled_shares(member, own, stays, other, coefficients, ordered, taps, pieces, scaling):
     count, _, _, head_size = own.shape
     groups = count // taps
     kept = head_size // (2 * pieces)
@@ -285,7 +286,7 @@
         compiler_params=pltpu.CompilerParams(vmem_limit_bytes=VMEM_SMALL),
         cost_estimate=pl.CostEstimate(flops=10**8, bytes_accessed=3 * 10**6, transcendentals=10**5),
         name="scaled_shares",
-    )(core, own, stays, other, coefficients, ordered)
+    )(member, own, stays, other, coefficients, ordered)
 
 
 def summed_kernel(terms, total):
@@ -375,17 +376,16 @@
     taps, heads, queries, head_size = disc_query.shape
     scaling = 0.5 / math.sqrt(head_size)
     members = lax.axis_size(SEQ)
-    core = lax.axis_index("core").astype(jnp.int32).reshape(1)
     member = lax.axis_index(SEQ).astype(jnp.int32).reshape(1)
     features, disc_query, disc_out, map_there = (
         pltpu.with_memory_space_constraint(whole, pltpu.HBM) for whole in (features, disc_query, disc_out, value_map)
     )
-    weights, ordered, stats = token_weights(core, features, disc_query, map_there, disc_out, scaling, members)
+    weights, ordered, stats = token_weights(member, label, features, disc_query, map_there, disc_out, scaling, members)
     every = exchanged(stats, SEQ)
     sent, stays = pooled_features(features, weights, heads // GROUP)
     other = lax.ppermute(sent, "core", [(0, 1), (1, 0)])
-    logit, coefficients = joined_stats(member, core, label, every, ordered.shape[0])
-    shares = scaled_shares(core, sent, stays, other, coefficients, ordered, taps, members // 2, scaling)
+    logit, coefficients = joined_stats(member, label, every, ordered.shape[0])
+    shares = scaled_shares(member, sent, stays, other, coefficients, ordered, taps, members // 2, scaling)
     terms = exchanged(shares.reshape(members, -1, head_size), ("yh", "yl", "x"))
     terms = exchanged(summed_parts(terms, lax.axis_size("zl")), ("zl",))
     terms = lax.all_gather(repeated_sum(terms, 1)[0], "zh")

time: 113 us -> 113 us (level)
  no operation moved by 1% of the time
where the time goes in v4:
time: 113 us
  blocking collectives  80.7 us (71%)
  starting transfers between devices  18.5 us (16%)
  Pallas kernels  10.3 us (9%)
  waiting for transfers between devices  1.98 us (2%)
  between operations  1.33 us (1%)
    all_gather x1, blocking collectives, on_device(): terms = lax.all_gather(repeated_sum(terms, 1)[0], 'zh')  43.7 us
    all_to_all x3, blocking collectives, exchanged(): return lax.all_to_all(parts, axes, 0, 0)  37 us
    all_to_all x1, starting transfers between devices, exchanged(): return lax.all_to_all(parts, axes, 0, 0)  16.5 us
    pallas_call x1, Pallas kernels, token_weights(): pl.pallas_call(functools.partial(weights_kernel, groups, scaling), out_sh...  5.06 us
    pallas_call x1, Pallas kernels, pooled_features(): pl.pallas_call(functools.partial(pooled_kernel, groups), out_shape=(jax.S...  2.44 us
  transfers between devices with their start and end apart: 2, of which 1 were waited for; matrix products, arithmetic and copies ran while one was open for 0% of the time, Pallas kernels for 3%

profile of v4, /device:TPU:8, one launch (start us, length us, event | category | flops | bytes accessed | tf_op | source)
XLA Modules:
  0.0 112.8 jit_solution(7723986642056476713)
XLA Ops:
  1.3 5.1 %token_weights.1 = (bf16[9,128,256]{2,1,0:T(8,128)(2,1)S(1)}, bf16[9,128,128]{2,1,0:T(8,128)(2,1)S(1)}, f32[16,32,128]{2,1,0:T(8,128)}) custom-call(s32[1]{0:T(128)} %bitcast.member.member_ref, s32[1]{0:T(128)S(6)} %copy.13.label, bf16[3,1,128,3072]{3,2,1,0:T(8,128)(2,1)} %feats_hbm.3, bf16[3,24,16,128]{3,2,1,0:T(8,128)(2,1)} %query_hbm.1, ...), custom_call_target="tpu_custom_call" | custom-call | flops 700000000 | bytes 4000000 | tf_op jit(solution)/shard_map/token_weights/pallas_call | solution.py:111
  6.4 16.5 %all-to-all-start = ((f32[16,32,128]{2,1,0:T(8,128)}), f32[16,32,128]{2,1,0:T(8,128)S(1)}, u32[]{:S(2)}, u32[]{:S(2)}) async-start(f32[16,32,128]{2,1,0:T(8,128)} %get-tuple-element.14), calls=%async_computation | async-start | bytes 524288 | tf_op jit(solution)/shard_map/all_to_all | solution.py:368
  22.8 2.4 %pooled_features.1 = (f32[9,3,64,128]{3,2,1,0:T(8,128)S(1)}, f32[9,64,128]{2,1,0:T(8,128)S(1)}) custom-call(bf16[3,1,128,3072]{3,2,1,0:T(8,128)(2,1)} %feats_hbm.3, bf16[9,128,256]{2,1,0:T(8,128)(2,1)S(1)} %get-tuple-element.16.weights), custom_call_target="tpu_custom_call" | custom-call | flops 80000000 | bytes 4000000 | tf_op jit(solution)/shard_map/pooled_features/pallas_call | solution.py:172
  25.3 2.1 %collective-permute-start = (f32[9,3,64,128]{3,2,1,0:T(8,128)S(1)}, f32[9,3,64,128]{3,2,1,0:T(8,128)S(1)}, u32[]{:S(2)}, u32[]{:S(2)}) collective-permute-start(f32[9,3,64,128]{3,2,1,0:T(8,128)S(1)} %get-tuple-element.17.own), channel_id=1, source_target_pairs={{0,1},{1,0},{2,3},{3,2},{4,5},{5,4},{6,7},{7,6},{8,9},{9,8},{10,11... | collective-permute-start | bytes 2654216 | tf_op jit(solution)/shard_map/ppermute | solution.py:386
  27.3 2.0 %all-to-all-done.every = f32[16,32,128]{2,1,0:T(8,128)S(1)} async-done(((f32[16,32,128]{2,1,0:T(8,128)}), f32[16,32,128]{2,1,0:T(8,128)S(1)}, u32[]{:S(2)}, u32[]{:S(2)}) %all-to-all-start) | async-done | bytes 262176 | tf_op jit(solution)/shard_map/all_to_all | solution.py:368
  29.3 0.7 joined_stats.1
  30.0 0.0 collective-permute-done.other
  30.0 0.0 copy-start
  30.0 1.3 %scaled_shares.1 = f32[2,8,88,128]{3,2,1,0:T(8,128)S(1)} custom-call(s32[1]{0:T(128)} %bitcast.member.member_ref, f32[9,3,64,128]{3,2,1,0:T(8,128)S(1)} %get-tuple-element.17.own, f32[9,64,128]{2,1,0:T(8,128)S(1)} %get-tuple-element.18.stays, f32[9,3,64,128]{3,2,1,0:T(8,128)S(1)} %collective-permute-done.other, ...), custom_call_target="tpu_custom_call" | custom-call | flops 100000000 | bytes 3000000 | tf_op jit(solution)/shard_map/scaled_shares/pallas_call | solution.py:280
  31.3 17.1 %all_to_all.20.terms = f32[16,88,128]{2,1,0:T(8,128)S(1)} all-to-all(f32[16,88,128]{2,1,0:T(8,128)S(1)} %bitcast.10), channel_id=1, replica_groups=mesh['zh'=8,'zl'=4,'yh'=2,'yl'=2,'x'=4,'core'=2] {'yh','yl','x'}, dimensions={0} | all-to-all | bytes 1441792 | tf_op jit(solution)/shard_map/all_to_all | solution.py:368
  48.4 8.1 %all_to_all.21.terms = f32[4,24,128]{2,1,0:T(8,128)S(1)} all-to-all(f32[4,24,128]{2,1,0:T(8,128)S(1)} %summed_parts.1), channel_id=1, replica_groups=mesh['zh'=8,'zl'=4,'yh'=2,'yl'=2,'x'=4,'core'=2] {'zl'}, dimensions={0} | all-to-all | bytes 98304 | tf_op jit(solution)/shard_map/all_to_all | solution.py:368
  56.5 43.7 %all_gather.3.terms = f32[8,24,128]{2,1,0:T(8,128)S(1)} all-gather(f32[1,24,128]{2,1,0:T(8,128)S(1)} %repeated_sum.2), channel_id=1, replica_groups=mesh['zh'=8,'zl'=4,'yh'=2,'yl'=2,'x'=4,'core'=2] {'zh'}, dimensions={0}, use_global_device_ids=true | all-gather | bytes 110592 | tf_op jit(solution)/shard_map/all_gather | solution.py:391
  100.2 11.9 %all_to_all.22 = f32[8,24,128]{2,1,0:T(8,128)S(1)} all-to-all(f32[8,24,128]{2,1,0:T(8,128)S(1)} %repeated_sum.3), channel_id=1, replica_groups=mesh['zh'=8,'zl'=4,'yh'=2,'yl'=2,'x'=4,'core'=2] {'zl','yh'}, dimensions={0} | all-to-all | bytes 196608 | tf_op jit(solution)/shard_map/all_to_all | solution.py:368
  112.1 0.0 copy-done
  112.1 0.8 final_outputs.1
  (3 shorter events, 0.1 us)
Async XLA Ops:
  6.4 23.0 %all-to-all-start = ((f32[16,32,128]{2,1,0:T(8,128)}), f32[16,32,128]{2,1,0:T(8,128)S(1)}, u32[]{:S(2)}, u32[]{:S(2)}) async-start(f32[16,32,128]{2,1,0:T(8,128)} %get-tuple-element.14), calls=%async_computation | async-start | bytes 524288 | tf_op jit(solution)/shard_map/all_to_all | solution.py:368
  25.3 4.7 %collective-permute-start = (f32[9,3,64,128]{3,2,1,0:T(8,128)S(1)}, f32[9,3,64,128]{3,2,1,0:T(8,128)S(1)}, u32[]{:S(2)}, u32[]{:S(2)}) collective-permute-start(f32[9,3,64,128]{3,2,1,0:T(8,128)S(1)} %get-tuple-element.17.own), channel_id=1, source_target_pairs={{0,1},{1,0},{2,3},{3,2},{4,5},{5,4},{6,7},{7,6},{8,9},{9,8},{10,11... | collective-permute-start | bytes 2654216 | tf_op jit(solution)/shard_map/ppermute | solution.py:386
  30.0 82.1 %copy-start = (bf16[3,128,128]{2,1,0:T(8,128)(2,1)S(1)}, bf16[3,128,128]{2,1,0:T(8,128)(2,1)}, u32[]{:S(2)}) copy-start(bf16[3,128,128]{2,1,0:T(8,128)(2,1)} %value_map.1) | copy-start | bytes 294916
